TPU v7x, 128 devices: a whole 4x4x4 slice. The times are simulated.
128 devices in a mesh: fsdp: 8 (over z_lo, x), dp: 4 (over y), cand: 4 (over z_hi, core).
Axes of the slice: x: 4, y: 4, z: 4 (z_hi: 2, z_lo: 2; z = z_hi * 2 + z_lo), core: 2. Of those that a mesh axis runs over, the one named last changes fastest.
Arguments:
- tokens: bfloat16 [640, 8192], P(('dp', 'cand'), 'fsdp'), may hold values from -6 to 6
- cotangent: bfloat16 [640, 8192], P(('dp', 'cand'), 'fsdp'), may hold values from -6 to 6
- bleu_gains: int32 [4, 8], P('dp', 'cand'), may hold values from 0 to 9600, as said below
- gate_weight: bfloat16 [8192, 29568], P('fsdp', ('dp', 'cand')), may hold values from -0.0625 to 0.0625
- up_weight: bfloat16 [8192, 29568], P('fsdp', ('dp', 'cand')), may hold values from -0.0625 to 0.0625
- down_weight: bfloat16 [29568, 8192], P(('dp', 'cand'), 'fsdp'), may hold values from -0.03125 to 0.03125
Outputs:
- layer_out: bfloat16 [640, 8192], P(('dp', 'cand'), 'fsdp')
- grad_tokens: bfloat16 [640, 8192], P(('dp', 'cand'), 'fsdp')
- grad_gate_weight: bfloat16 [8192, 29568], P('fsdp', ('dp', 'cand'))
- grad_up_weight: bfloat16 [8192, 29568], P('fsdp', ('dp', 'cand'))
- grad_down_weight: bfloat16 [29568, 8192], P(('dp', 'cand'), 'fsdp')
Inputs may be any that keep to these rules, and one draw needn't show every extreme that they name: `bleu_gains`: BLEU gain of a candidate in parts per ten thousand.
All inputs are finite; a program needn't handle non-finite values.
Results may differ from a plain program's by a relative error of at most 0.0058.
Values may be sent and summed in bfloat16 or wider, within the bound.
No kernel may reach another device: no remote copies, remote signals or barrier semaphores. Data moves between devices by JAX's collectives and lax.ppermute only.
A program may use at most 128 MiB of HBM per device.

v0:
```python
import jax
import jax.numpy as jnp
from jax import lax
from jax.sharding import PartitionSpec as P

CANDS = 8


def swiglu_backward(back_sum, gate_sum, up_sum):
    sigmoid_gate = jax.nn.sigmoid(gate_sum)
    grad_gate = (back_sum * up_sum * sigmoid_gate * (1.0 + gate_sum * (1.0 - sigmoid_gate))).astype(
        jnp.bfloat16
    )
    grad_up = (back_sum * (gate_sum * sigmoid_gate)).astype(jnp.bfloat16)
    return (grad_gate, grad_up)


def swiglu_forward(gate_sum, up_sum):
    return (gate_sum * jax.nn.sigmoid(gate_sum) * up_sum).astype(jnp.bfloat16)


def on_device(tokens, cotangent, bleu_gains, gate_weight, up_weight, down_weight):
    own_rows = tokens.shape[0]
    seq_len = own_rows // bleu_gains.size
    contract_cols = (((1,), (1,)), ((), ()))
    contract_rows = (((0,), (0,)), ((), ()))
    tok_all = lax.all_gather(tokens, ("dp", "cand"), axis=0, tiled=True)
    shifted = (bleu_gains + 1).astype(jnp.float32)
    totals = lax.psum(jnp.sum(shifted, axis=1), "cand")
    row_scale = jnp.repeat((CANDS * shifted / totals[:, None]).reshape(-1), seq_len)
    grad_own = (row_scale[:, None] * cotangent).astype(jnp.bfloat16)
    grad_all = lax.all_gather(grad_own, ("dp", "cand"), axis=0, tiled=True)
    gate_part = jnp.dot(tok_all, gate_weight, preferred_element_type=jnp.float32)
    up_part = jnp.dot(tok_all, up_weight, preferred_element_type=jnp.float32)
    gate_sum, up_sum = lax.psum((gate_part, up_part), "fsdp")
    hidden = swiglu_forward(gate_sum, up_sum)
    layer_out = lax.psum_scatter(
        jnp.dot(hidden, down_weight, preferred_element_type=jnp.float32),
        ("dp", "cand"),
        scatter_dimension=0,
        tiled=True,
    ).astype(jnp.bfloat16)
    back_part = lax.dot_general(
        grad_all, down_weight, contract_cols, preferred_element_type=jnp.float32
    )
    back_sum = lax.psum(back_part, "fsdp")
    grad_gate, grad_up = swiglu_backward(back_sum, gate_sum, up_sum)
    grad_down_weight = lax.dot_general(
        hidden, grad_all, contract_rows, preferred_element_type=jnp.float32
    ).astype(jnp.bfloat16)
    grad_gate_weight = lax.dot_general(
        tok_all, grad_gate, contract_rows, preferred_element_type=jnp.float32
    ).astype(jnp.bfloat16)
    grad_up_weight = lax.dot_general(
        tok_all, grad_up, contract_rows, preferred_element_type=jnp.float32
    ).astype(jnp.bfloat16)
    from_gate = lax.dot_general(
        grad_gate, gate_weight, contract_cols, preferred_element_type=jnp.float32
    )
    from_up = lax.dot_general(grad_up, up_weight, contract_cols, preferred_element_type=jnp.float32)
    grad_tokens = lax.psum_scatter(
        from_gate + from_up, ("dp", "cand"), scatter_dimension=0, tiled=True
    ).astype(jnp.bfloat16)
    return (layer_out, grad_tokens, grad_gate_weight, grad_up_weight, grad_down_weight)


def solution(mesh):
    return jax.shard_map(
        on_device,
        mesh=mesh,
        in_specs=(
            P(("dp", "cand"), "fsdp"),
            P(("dp", "cand"), "fsdp"),
            P("dp", "cand"),
            P("fsdp", ("dp", "cand")),
            P("fsdp", ("dp", "cand")),
            P(("dp", "cand"), "fsdp"),
        ),
        out_specs=(
            P(("dp", "cand"), "fsdp"),
            P(("dp", "cand"), "fsdp"),
            P("fsdp", ("dp", "cand")),
            P("fsdp", ("dp", "cand")),
            P(("dp", "cand"), "fsdp"),
        ),
        check_vma=False,
    )
```

profile of v0, /device:TPU:0, one launch (start us, length us, event | category | flops | bytes accessed | tf_op | source)
XLA Modules:
  0.0 578.3 jit_solution(13196504414203694526)
XLA Ops:
  7.2 0.0 all-gather.3.cloned.1.call-start
  7.2 0.7 all-gather.3.cloned.1.call-update
  7.9 0.0 all-gather.5.cloned.1.call-start
  7.9 1.3 convert_reduce_fusion
  9.2 11.5 %psum.30 = f32[]{:T(128)} all-reduce(f32[]{:T(128)} %convert_reduce_fusion), channel_id=1, replica_groups=mesh['fsdp'=8,'dp'=4,'cand'=4] {'cand'}, use_global_device_ids=true, to_apply=%region_4.0 | all-reduce | flops 1 | bytes 8 | tf_op jit(solution)/shard_map/psum | solution.py:29
  20.7 1.3 divide_bitcast_fusion
  22.0 0.1 broadcast_in_dim.4
  22.1 0.1 mul.38
  22.1 1.6 multiply_convert_fusion.3
  23.7 0.0 all-gather.5.cloned.1.call-update
  23.8 0.0 all-reduce.3.cloned.1.call-start
  23.8 35.1 %all-gather.3.cloned.1.call-done = bf16[640,1024]{1,0:T(8,128)(2,1)} async-done(((bf16[40,1024]{1,0:T(8,128)(2,1)}), bf16[640,1024]{1,0:T(8,128)(2,1)}) %all-gather.3.cloned.1.call-update) | async-done | bytes 1310736 | tf_op jit(solution)/shard_map/all_gather | solution.py:27
  58.9 0.0 copy-start.4
  58.9 0.0 copy-start.5
  58.9 7.9 %fusion.2 = f32[640,1848]{0,1:T(8,128)} fusion(bf16[640,1024]{1,0:T(8,128)(2,1)} %all-gather.3.cloned.1.call-done, bf16[1024,1848]{0,1:T(8,128)(2,1)} %param.10), kind=kOutput, calls=%fused_computation.13 | convolution fusion | flops 2422210560 | bytes 9826304 | tf_op jit(solution)/shard_map/dot_general | solution.py:34
  66.8 0.0 copy-done.4
  66.8 0.0 copy-done.5
  66.8 4.9 fusion.1
  71.7 34.9 %all-gather.5.cloned.1.call-done = bf16[640,1024]{1,0:T(8,128)(2,1)} async-done(((bf16[40,1024]{1,0:T(8,128)(2,1)}), bf16[640,1024]{1,0:T(8,128)(2,1)}) %all-gather.5.cloned.1.call-update) | async-done | bytes 1310736 | tf_op jit(solution)/shard_map/all_gather | solution.py:32
  106.5 7.9 %fusion.4 = f32[640,1848]{0,1:T(8,128)} fusion(bf16[640,1024]{1,0:T(8,128)(2,1)} %all-gather.5.cloned.1.call-done, bf16[1848,1024]{1,0:T(8,128)(2,1)} %param.11), kind=kOutput, calls=%fused_computation.15 | convolution fusion | flops 2422210560 | bytes 9826304 | tf_op jit(solution)/shard_map/dot_general | solution.py:43
  114.4 0.0 all-reduce.3.cloned.1.call-update
  114.4 0.0 reduce-scatter.3.cloned.1.call-start
  114.5 293.4 %all-reduce.3.cloned.1.call-done = (f32[640,1848]{0,1:T(8,128)}, f32[640,1848]{0,1:T(8,128)}, f32[640,1848]{0,1:T(8,128)}) async-done(((f32[640,1848]{0,1:T(8,128)}, f32[640,1848]{0,1:T(8,128)}, f32[640,1848]{0,1:T(8,128)}), (f32[640,1848]{0,1:T(8,128)}, f32[640,1848]{0,1:T(8,128)}, f32[640,1848]{0,1:T(8,128)})) %all-reduce.3.cloned.1.call-update) | async-done | bytes 14192656 | tf_op jit(solution)/shard_map/psum | solution.py:35
  407.8 0.0 copy-start.3
  407.8 7.6 %multiply_convert_fusion = (bf16[640,1848]{0,1:T(8,128)(2,1)S(1)}, bf16[640,1848]{0,1:T(8,128)(2,1)}, bf16[640,1848]{0,1:T(8,128)(2,1)S(1)}) fusion(f32[640,1848]{0,1:T(8,128)} %get-tuple-element.7, f32[640,1848]{0,1:T(8,128)} %get-tuple-element.6, f32[640,1848]{0,1:T(8,128)} %get-tuple-element.5), kind=kLoop, calls=%fused_computation | loop fusion | flops 17740800 | bytes 21288960 | tf_op jit(solution)/shard_map/convert_element_type | solution.py:14
  415.4 0.0 copy-start.2
  415.4 1.4 copy-done.2
  416.8 0.0 copy-done.3
  416.8 4.5 fusion.3
  421.3 0.0 reduce-scatter.3.cloned.1.call-update
  421.3 0.2 reduce-scatter.5.cloned.1.call-start
  421.6 0.0 copy-start
  421.6 5.9 %fusion.5 = f32[640,1024]{1,0:T(8,128)S(1)} fusion(bf16[640,1848]{0,1:T(8,128)(2,1)} %get-tuple-element.9, bf16[1024,1848]{0,1:T(8,128)(2,1)} %param.9), kind=kOutput, calls=%fused_computation.16 | convolution fusion | flops 2422210560 | bytes 8771584 | tf_op jit(solution)/shard_map/dot_general | solution.py:57
  427.5 0.0 copy-done
  427.5 4.5 convolution_add_fusion
  432.0 0.0 reduce-scatter.5.cloned.1.call-update
  432.0 0.0 copy-start.6
  432.1 7.3 %convolution_convert_fusion = bf16[1848,1024]{1,0:T(8,128)(2,1)} fusion(bf16[640,1848]{0,1:T(8,128)(2,1)} %copy-done.2, bf16[640,1024]{1,0:T(8,128)(2,1)} %all-gather.5.cloned.1.call-done), kind=kOutput, calls=%fused_computation.7 | convolution fusion | flops 2424102912 | bytes 7460864 | tf_op jit(solution)/shard_map/dot_general | solution.py:48
  439.3 0.0 copy-done.6
  439.3 0.0 copy-start.1
  439.3 4.6 convert_bitcast_fusion
  443.9 0.0 copy-done.1
  443.9 4.6 convert_bitcast_fusion.1
  448.5 45.2 %reduce-scatter.3.cloned.1.call-done = f32[40,1024]{1,0:T(8,128)} async-done(((f32[640,1024]{1,0:T(8,128)}), f32[40,1024]{1,0:T(8,128)}) %reduce-scatter.3.cloned.1.call-update) | async-done | bytes 163856 | tf_op jit(solution)/shard_map/reduce_scatter | solution.py:37
  493.7 1.6 convert_element_type.40
  495.3 75.0 %reduce-scatter.5.cloned.1.call-done = f32[40,1024]{1,0:T(8,128)} async-done(((f32[640,1024]{1,0:T(8,128)}), f32[40,1024]{1,0:T(8,128)}) %reduce-scatter.5.cloned.1.call-update) | async-done | bytes 163856 | tf_op jit(solution)/shard_map/reduce_scatter | solution.py:61
  570.2 1.6 convert_element_type.46
Async XLA Ops:
  7.2 51.8 %all-gather.3.cloned.1.call-start = ((), (), s32[]{:S(2)}) async-start(), calls=%async_computation.2 | async-start | bytes 1392640 | tf_op jit(solution)/shard_map/all_gather | solution.py:27
  7.9 98.6 %all-gather.5.cloned.1.call-start = ((), (), s32[]{:S(2)}) async-start(), calls=%async_computation.4 | async-start | bytes 1392640 | tf_op jit(solution)/shard_map/all_gather | solution.py:32
  23.8 384.1 %all-reduce.3.cloned.1.call-start = ((), (), s32[]{:S(2)}) async-start(), calls=%async_computation.6 | async-start | bytes 28385280 | tf_op jit(solution)/shard_map/psum | solution.py:35
  58.9 7.9 %copy-start.4 = (bf16[1024,1848]{0,1:T(8,128)(2,1)S(1)}, bf16[1024,1848]{0,1:T(8,128)(2,1)}, u32[]{:S(2)}) copy-start(bf16[1024,1848]{0,1:T(8,128)(2,1)} %param.9) | copy-start | bytes 11354116
  58.9 7.9 %copy-start.5 = (bf16[640,1024]{1,0:T(8,128)(2,1)S(1)}, bf16[640,1024]{1,0:T(8,128)(2,1)}, u32[]{:S(2)}) copy-start(bf16[640,1024]{1,0:T(8,128)(2,1)} %all-gather.3.cloned.1.call-done) | copy-start | bytes 3932164
  114.4 379.3 %reduce-scatter.3.cloned.1.call-start = ((), (), s32[]{:S(2)}) async-start(), calls=%async_computation.3 | async-start | bytes 2785280 | tf_op jit(solution)/shard_map/reduce_scatter | solution.py:37
  407.8 9.0 %copy-start.3 = (bf16[1848,1024]{1,0:T(8,128)(2,1)S(1)}, bf16[1848,1024]{1,0:T(8,128)(2,1)}, u32[]{:S(2)}) copy-start(bf16[1848,1024]{1,0:T(8,128)(2,1)} %param.11) | copy-start | bytes 11354116
  415.4 1.4 copy-start.2
  421.3 148.9 %reduce-scatter.5.cloned.1.call-start = ((), (), s32[]{:S(2)}) async-start(), calls=%async_computation.5 | async-start | bytes 2785280 | tf_op jit(solution)/shard_map/reduce_scatter | solution.py:61
  421.6 5.9 %copy-start = (bf16[1024,1848]{0,1:T(8,128)(2,1)S(1)}, bf16[1024,1848]{0,1:T(8,128)(2,1)}, u32[]{:S(2)}) copy-start(bf16[1024,1848]{0,1:T(8,128)(2,1)} %param.10) | copy-start | bytes 11354116
  432.0 7.3 %copy-start.6 = (bf16[640,1024]{1,0:T(8,128)(2,1)S(1)}, bf16[640,1024]{1,0:T(8,128)(2,1)}, u32[]{:S(2)}) copy-start(bf16[640,1024]{1,0:T(8,128)(2,1)} %all-gather.3.cloned.1.call-done) | copy-start | bytes 3932164
  439.3 4.6 copy-start.1
Sparse Core Ops, SparseCore 0:
  10.4 48.4 all-gather.2
  61.9 44.5 all-gather.4
  114.5 293.2 all-reduce.2
  421.4 72.2 reduce-scatter.2
  498.1 72.1 reduce-scatter.4
where the time goes:
time: 579 us; the launch traced here: 578 us
  waiting for transfers between devices  484 us (84%)
  matrix products  51.9 us (9%)
  other arithmetic  14.9 us (3%)
  between operations  13.8 us (2%)
  blocking collectives  11.5 us (2%)
    psum x1, waiting for transfers between devices, on_device(): gate_sum, up_sum = lax.psum((gate_part, up_part), 'fsdp')  293 us
    reduce_scatter x1, waiting for transfers between devices, on_device(): lax.psum_scatter(from_gate + from_up, ('dp', 'cand'), scatter_dimension=0...  75 us
    reduce_scatter x1, waiting for transfers between devices, on_device(): lax.psum_scatter(jnp.dot(hidden, down_weight, preferred_element_type=jnp....  45.2 us
    all_gather x1, waiting for transfers between devices, on_device(): tok_all = lax.all_gather(tokens, ('dp', 'cand'), axis=0, tiled=True)  35.1 us
    all_gather x1, waiting for transfers between devices, on_device(): grad_all = lax.all_gather(grad_own, ('dp', 'cand'), axis=0, tiled=True)  34.9 us
  transfers between devices with their start and end apart: 5, of which 5 were waited for; matrix products, arithmetic and copies ran while one was open for 8% of the time, Pallas kernels for 0%

commit v1 on v0

--- a/solution.py
+++ b/solution.py
@@ -24,7 +24,10 @@
     seq_len = own_rows // bleu_gains.size
     contract_cols = (((1,), (1,)), ((), ()))
     contract_rows = (((0,), (0,)), ((), ()))
-    tok_all = lax.all_gather(tokens, ("dp", "cand"), axis=0, tiled=True)
+    tok_all = jnp.concatenate(
+        lax.all_to_all(jnp.stack([tokens] * lax.axis_size(("dp", "cand"))), ("dp", "cand"), 0, 0),
+        axis=0,
+    )
     shifted = (bleu_gains + 1).astype(jnp.float32)
     totals = lax.psum(jnp.sum(shifted, axis=1), "cand")
     row_scale = jnp.repeat((CANDS * shifted / totals[:, None]).reshape(-1), seq_len)

time: 579 us -> 558 us (0.964)
  waiting for transfers between devices: 484 us -> 456 us
  starting transfers between devices: 0.38 us -> 8.32 us
    all_gather x1 -> x0, waiting for transfers between devices: 35.1 us -> none  [on_device(): tok_all = lax.all_gather(tokens, ('dp', 'cand'), axis=0, tiled=True)]
    all_to_all x0 -> x1, starting transfers between devices: none -> 7.97 us  [on_device(): lax.all_to_all(jnp.stack([tokens] * lax.axis_size(('dp', 'cand'))), ('dp'...]
    all_to_all x0 -> x1, waiting for transfers between devices: none -> 7.07 us  [on_device(): lax.all_to_all(jnp.stack([tokens] * lax.axis_size(('dp', 'cand'))), ('dp'...]
  transfers between devices with their start and end apart: 5 -> 5, of which waited for: 5 -> 5; matrix products, arithmetic and copies ran while one was open for 8% -> 7% of each run, Pallas kernels for 0% -> 0%
where the time goes in v1:
time: 558 us
  waiting for transfers between devices  456 us (82%)
  matrix products  50.6 us (9%)
  between operations  13.9 us (2%)
  other arithmetic  13.4 us (2%)
  blocking collectives  12.1 us (2%)
  starting transfers between devices  8.32 us (1%)
    psum x1, waiting for transfers between devices, on_device(): gate_sum, up_sum = lax.psum((gate_part, up_part), 'fsdp')  293 us
    reduce_scatter x1, waiting for transfers between devices, on_device(): lax.psum_scatter(from_gate + from_up, ('dp', 'cand'), scatter_dimension=0...  75 us
    reduce_scatter x1, waiting for transfers between devices, on_device(): lax.psum_scatter(jnp.dot(hidden, down_weight, preferred_element_type=jnp....  46.3 us
    all_gather x1, waiting for transfers between devices, on_device(): grad_all = lax.all_gather(grad_own, ('dp', 'cand'), axis=0, tiled=True)  34 us
    psum x1, blocking collectives, on_device(): totals = lax.psum(jnp.sum(shifted, axis=1), 'cand')  12.1 us
  transfers between devices with their start and end apart: 5, of which 5 were waited for; matrix products, arithmetic and copies ran while one was open for 7% of the time, Pallas kernels for 0%

profile of v1, /device:TPU:0, one launch (start us, length us, event | category | flops | bytes accessed | tf_op | source)
XLA Modules:
  0.0 557.8 jit_solution(9164979560017737502)
XLA Ops:
  7.2 0.0 copy-start.10
  7.2 0.0 copy-start.6
  7.2 1.3 convert_reduce_fusion
  8.5 2.1 stack.2
  10.6 8.0 %all-to-all-start = ((bf16[16,40,1024]{2,1,0:T(8,128)(2,1)}), bf16[16,40,1024]{2,1,0:T(8,128)(2,1)S(1)}, u32[]{:S(2)}, u32[]{:S(2)}) async-start(bf16[16,40,1024]{2,1,0:T(8,128)(2,1)} %stack.2), calls=%async_computation | async-start | bytes 2621440 | tf_op jit(solution)/shard_map/all_to_all | solution.py:28
  18.6 0.0 all-gather.2.cloned.1.call-start
  18.6 12.1 %psum.30 = f32[]{:T(128)} all-reduce(f32[]{:T(128)} %convert_reduce_fusion), channel_id=1, replica_groups=mesh['fsdp'=8,'dp'=4,'cand'=4] {'cand'}, use_global_device_ids=true, to_apply=%region_4.0 | all-reduce | flops 1 | bytes 8 | tf_op jit(solution)/shard_map/psum | solution.py:32
  30.7 0.0 copy-done.10
  30.7 0.7 divide_bitcast_fusion
  31.4 0.1 broadcast_in_dim.4
  31.4 0.1 mul.38
  31.5 0.0 copy-done.6
  31.5 0.7 multiply_convert_fusion.3
  32.2 0.0 all-gather.2.cloned.1.call-update
  32.3 0.0 all-reduce.3.cloned.1.call-start
  32.3 7.1 %all-to-all-done = bf16[16,40,1024]{2,1,0:T(8,128)(2,1)S(1)} async-done(((bf16[16,40,1024]{2,1,0:T(8,128)(2,1)}), bf16[16,40,1024]{2,1,0:T(8,128)(2,1)S(1)}, u32[]{:S(2)}, u32[]{:S(2)}) %all-to-all-start) | async-done | bytes 1310752 | tf_op jit(solution)/shard_map/all_to_all | solution.py:28
  39.4 7.9 %fusion.2 = f32[640,1848]{0,1:T(8,128)} fusion(bf16[640,1024]{1,0:T(8,128)(2,1)S(1)} %bitcast.25, bf16[1024,1848]{0,1:T(8,128)(2,1)} %param.10), kind=kOutput, calls=%fused_computation.13 | convolution fusion | flops 2422210560 | bytes 9826304 | tf_op jit(solution)/shard_map/dot_general | solution.py:37
  47.2 0.0 copy-done.4
  47.2 0.0 copy-done.8
  47.2 4.8 fusion.1
  52.0 34.0 %all-gather.2.cloned.1.call-done = bf16[640,1024]{1,0:T(8,128)(2,1)} async-done(((bf16[40,1024]{1,0:T(8,128)(2,1)}), bf16[640,1024]{1,0:T(8,128)(2,1)}) %all-gather.2.cloned.1.call-update) | async-done | bytes 1310736 | tf_op jit(solution)/shard_map/all_gather | solution.py:35
  86.1 7.8 %fusion.4 = f32[640,1848]{0,1:T(8,128)} fusion(bf16[640,1024]{1,0:T(8,128)(2,1)} %all-gather.2.cloned.1.call-done, bf16[1848,1024]{1,0:T(8,128)(2,1)} %param.11), kind=kOutput, calls=%fused_computation.15 | convolution fusion | flops 2422210560 | bytes 9826304 | tf_op jit(solution)/shard_map/dot_general | solution.py:46
  93.9 0.0 all-reduce.3.cloned.1.call-update
  93.9 0.0 reduce-scatter.3.cloned.1.call-start
  94.0 293.4 %all-reduce.3.cloned.1.call-done = (f32[640,1848]{0,1:T(8,128)}, f32[640,1848]{0,1:T(8,128)}, f32[640,1848]{0,1:T(8,128)}) async-done(((f32[640,1848]{0,1:T(8,128)}, f32[640,1848]{0,1:T(8,128)}, f32[640,1848]{0,1:T(8,128)}), (f32[640,1848]{0,1:T(8,128)}, f32[640,1848]{0,1:T(8,128)}, f32[640,1848]{0,1:T(8,128)})) %all-reduce.3.cloned.1.call-update) | async-done | bytes 14192656 | tf_op jit(solution)/shard_map/psum | solution.py:38
  387.3 7.6 %multiply_convert_fusion = (bf16[640,1848]{0,1:T(8,128)(2,1)S(1)}, bf16[640,1848]{0,1:T(8,128)(2,1)}, bf16[640,1848]{0,1:T(8,128)(2,1)S(1)}) fusion(f32[640,1848]{0,1:T(8,128)} %get-tuple-element.7, f32[640,1848]{0,1:T(8,128)} %get-tuple-element.6, f32[640,1848]{0,1:T(8,128)} %get-tuple-element.5), kind=kLoop, calls=%fused_computation | loop fusion | flops 17740800 | bytes 21288960 | tf_op jit(solution)/shard_map/convert_element_type | solution.py:14
  394.9 1.5 copy-done.1
  396.3 0.0 copy-done.7
  396.3 4.4 fusion.3
  400.8 0.0 reduce-scatter.3.cloned.1.call-update
  400.8 0.2 reduce-scatter.5.cloned.1.call-start
  401.0 0.0 copy-start
  401.0 5.9 %fusion.5 = f32[640,1024]{1,0:T(8,128)S(1)} fusion(bf16[640,1848]{0,1:T(8,128)(2,1)} %get-tuple-element.9, bf16[1024,1848]{0,1:T(8,128)(2,1)} %param.9), kind=kOutput, calls=%fused_computation.16 | convolution fusion | flops 2422210560 | bytes 8771584 | tf_op jit(solution)/shard_map/dot_general | solution.py:60
  406.9 0.0 copy-done
  406.9 4.6 convolution_add_fusion
  411.5 0.0 reduce-scatter.5.cloned.1.call-update
  411.5 0.0 copy-start.3
  411.6 0.0 copy-start.5
  411.6 6.1 %convert_bitcast_fusion = bf16[1024,1848]{0,1:T(8,128)(2,1)} fusion(bf16[640,1848]{0,1:T(8,128)(2,1)S(1)} %get-tuple-element.8, bf16[640,1024]{1,0:T(8,128)(2,1)} %bitcast.27), kind=kOutput, calls=%fused_computation.5 | convolution fusion | flops 2424102912 | bytes 7460864 | tf_op jit(solution)/shard_map/dot_general | solution.py:57
  417.7 0.0 copy-done.3
  417.7 0.0 copy-done.5
  417.7 0.0 copy-start.9
  417.7 4.6 convert_bitcast_fusion.1
  422.3 4.6 convolution_convert_fusion
  426.8 46.3 %reduce-scatter.3.cloned.1.call-done = f32[40,1024]{1,0:T(8,128)} async-done(((f32[640,1024]{1,0:T(8,128)}), f32[40,1024]{1,0:T(8,128)}) %reduce-scatter.3.cloned.1.call-update) | async-done | bytes 163856 | tf_op jit(solution)/shard_map/reduce_scatter | solution.py:40
  473.2 1.6 convert_element_type.40
  474.7 75.0 %reduce-scatter.5.cloned.1.call-done = f32[40,1024]{1,0:T(8,128)} async-done(((f32[640,1024]{1,0:T(8,128)}), f32[40,1024]{1,0:T(8,128)}) %reduce-scatter.5.cloned.1.call-update) | async-done | bytes 163856 | tf_op jit(solution)/shard_map/reduce_scatter | solution.py:64
  549.7 1.6 convert_element_type.46
  (7 shorter events, 0.0 us)
Async XLA Ops:
  7.2 23.5 %copy-start.10 = (s32[1,2]{1,0:T(1,128)S(1)}, s32[1,2]{1,0:T(1,128)}, u32[]{:S(2)}) copy-start(s32[1,2]{1,0:T(1,128)} %param.8) | copy-start | bytes 28
  7.2 24.3 %copy-start.6 = (bf16[40,1024]{1,0:T(8,128)(2,1)S(1)}, bf16[40,1024]{1,0:T(8,128)(2,1)}, u32[]{:S(2)}) copy-start(bf16[40,1024]{1,0:T(8,128)(2,1)} %param.7) | copy-start | bytes 245764
  10.6 28.8 %all-to-all-start = ((bf16[16,40,1024]{2,1,0:T(8,128)(2,1)}), bf16[16,40,1024]{2,1,0:T(8,128)(2,1)S(1)}, u32[]{:S(2)}, u32[]{:S(2)}) async-start(bf16[16,40,1024]{2,1,0:T(8,128)(2,1)} %stack.2), calls=%async_computation | async-start | bytes 2621440 | tf_op jit(solution)/shard_map/all_to_all | solution.py:28
  18.6 67.5 %all-gather.2.cloned.1.call-start = ((), (), s32[]{:S(2)}) async-start(), calls=%async_computation.4 | async-start | bytes 1392640 | tf_op jit(solution)/shard_map/all_gather | solution.py:35
  32.3 355.1 %all-reduce.3.cloned.1.call-start = ((), (), s32[]{:S(2)}) async-start(), calls=%async_computation.6 | async-start | bytes 28385280 | tf_op jit(solution)/shard_map/psum | solution.py:38
  39.4 7.9 %copy-start.4 = (bf16[16,40,1024]{2,1,0:T(8,128)(2,1)}, bf16[16,40,1024]{2,1,0:T(8,128)(2,1)S(1)}, u32[]{:S(2)}) copy-start(bf16[16,40,1024]{2,1,0:T(8,128)(2,1)S(1)} %all-to-all-done) | copy-start | bytes 3932164
  39.4 7.9 %copy-start.8 = (bf16[1024,1848]{0,1:T(8,128)(2,1)S(1)}, bf16[1024,1848]{0,1:T(8,128)(2,1)}, u32[]{:S(2)}) copy-start(bf16[1024,1848]{0,1:T(8,128)(2,1)} %param.9) | copy-start | bytes 11354116
  93.9 379.3 %reduce-scatter.3.cloned.1.call-start = ((), (), s32[]{:S(2)}) async-start(), calls=%async_computation.3 | async-start | bytes 2785280 | tf_op jit(solution)/shard_map/reduce_scatter | solution.py:40
  387.3 9.0 %copy-start.7 = (bf16[1848,1024]{1,0:T(8,128)(2,1)S(1)}, bf16[1848,1024]{1,0:T(8,128)(2,1)}, u32[]{:S(2)}) copy-start(bf16[1848,1024]{1,0:T(8,128)(2,1)} %param.11) | copy-start | bytes 11354116
  394.9 1.5 copy-start.1
  400.8 149.0 %reduce-scatter.5.cloned.1.call-start = ((), (), s32[]{:S(2)}) async-start(), calls=%async_computation.5 | async-start | bytes 2785280 | tf_op jit(solution)/shard_map/reduce_scatter | solution.py:64
  401.0 5.9 %copy-start = (bf16[1024,1848]{0,1:T(8,128)(2,1)S(1)}, bf16[1024,1848]{0,1:T(8,128)(2,1)}, u32[]{:S(2)}) copy-start(bf16[1024,1848]{0,1:T(8,128)(2,1)} %param.10) | copy-start | bytes 11354116
  411.5 6.1 %copy-start.3 = (bf16[640,1848]{0,1:T(8,128)(2,1)S(1)}, bf16[640,1848]{0,1:T(8,128)(2,1)}, u32[]{:S(2)}) copy-start(bf16[640,1848]{0,1:T(8,128)(2,1)} %get-tuple-element.9) | copy-start | bytes 7096324
  411.6 6.1 %copy-start.5 = (bf16[16,40,1024]{2,1,0:T(8,128)(2,1)S(1)}, bf16[16,40,1024]{2,1,0:T(8,128)(2,1)}, u32[]{:S(2)}) copy-start(bf16[16,40,1024]{2,1,0:T(8,128)(2,1)} %copy-done.4) | copy-start | bytes 3932164
  417.7 4.6 copy-start.2
  417.7 4.6 copy-start.9
Sparse Core Ops, SparseCore 0:
  32.4 53.6 all-gather.1
  94.0 293.2 all-reduce.2
  400.9 72.2 reduce-scatter.2
  477.5 72.1 reduce-scatter.4
